TPU v7x, 32 devices: a whole 2x2x4 slice. The times are simulated.
32 devices in a mesh: dp: 8 (over y, x, core), seq: 4 (over z).
Axes of the slice: x: 2, y: 2, z: 4, core: 2. Of those that a mesh axis runs over, the one named last changes fastest.
Arguments:
- query: bfloat16 [8, 512, 512], P('dp', 'seq'), may hold values from -8 to 8
- key: bfloat16 [8, 512, 512], P('dp', 'seq'), may hold values from -8 to 8
- value: bfloat16 [8, 512, 512], P('dp', 'seq'), may hold values from -6 to 6
- out_ctx: bfloat16 [8, 512, 512], P('dp', 'seq'), may hold values from -6 to 6
- d_out: bfloat16 [8, 512, 512], P('dp', 'seq'), may hold values from -6 to 6
- score_bias: float32 [4, 4], P('seq'), may hold values from -2 to 2
- block_list: int32 [4, 4, 4], P('seq'), may hold values from 0 to 3, as said below
- block_count: int32 [4, 4], P('seq'), may hold values from 1 to 4, as said below
- hit_count: int32 [8], P('dp'), may hold values from 128 to 512, as said below
Outputs:
- d_query: bfloat16 [8, 512, 512], P('dp', 'seq')
- d_key: bfloat16 [8, 512, 512], P('dp', 'seq')
- d_value: bfloat16 [8, 512, 512], P('dp', 'seq')
- d_bias: float32 [4, 4], P('seq')
Inputs may be any that keep to these rules, and one draw needn't show every extreme that they name: Each list block_list[h, q] holds 4 different key blocks, the first being block q itself; only its first block_count[h, q] entries are used. `block_count`: some head has a list with all 4 entries used. `hit_count`: some event has all 512 hits real.
All inputs are finite; a program needn't handle non-finite values.
Results may differ from a plain program's by a relative error of at most 0.0049.
Values may be sent and summed in bfloat16 or wider, within the bound.
A program may use at most 64 MiB of HBM per device.

v0:
```python
import math
import jax
import jax.numpy as jnp
from jax import lax
from jax.sharding import PartitionSpec as P

MASKED = -1000000000.0


def head_grads(
    query_head,
    key_head,
    value_head,
    grad_head,
    delta_head,
    bias_row,
    list_rows,
    count_row,
    hit_limit,
    slot_end,
):
    nblocks = list_rows.shape[0]
    hits, head_dim = query_head.shape
    block = hits // nblocks
    scale = 1.0 / math.sqrt(head_dim)
    query_blocks = query_head.reshape(nblocks, block, head_dim)
    key_blocks = key_head.reshape(nblocks, block, head_dim)
    value_blocks = value_head.reshape(nblocks, block, head_dim)
    grad_blocks = grad_head.reshape(nblocks, block, head_dim)
    delta_blocks = delta_head.reshape(nblocks, block)
    within = jnp.arange(block, dtype=jnp.int32)
    block_ids = jnp.arange(nblocks, dtype=jnp.int32)
    row_valid = (jnp.arange(hits, dtype=jnp.int32) < hit_limit).reshape(nblocks, block)

    def slot_scores(slot_at):
        chosen = lax.dynamic_index_in_dim(list_rows, slot_at, axis=1, keepdims=False)
        key_taken = jnp.take(key_blocks, chosen, axis=0)
        matched = chosen[:, None] == block_ids[None, :]
        shift = jnp.sum(jnp.where(matched, bias_row[None, :], 0.0), axis=1)
        scores = (
            jnp.einsum("qid,qjd->qij", query_blocks, key_taken, preferred_element_type=jnp.float32)
            * scale
        )
        scores = scores + shift[:, None, None]
        key_real = chosen[:, None] * block + within[None, :] < hit_limit
        allowed = (slot_at < count_row)[:, None, None] & key_real[:, None, :]
        return (jnp.where(allowed, scores, MASKED), allowed, chosen, matched, key_taken)

    def first_pass(slot_at, state_now):
        row_top, row_total = state_now
        scores = slot_scores(slot_at)[0]
        new_top = jnp.maximum(row_top, jnp.max(scores, axis=2))
        row_total = row_total * jnp.exp(row_top - new_top) + jnp.sum(
            jnp.exp(scores - new_top[:, :, None]), axis=2
        )
        return (new_top, row_total)

    start_top = jnp.full((nblocks, block), -1e30, jnp.float32)
    start_total = jnp.zeros((nblocks, block), jnp.float32)
    row_top, row_total = lax.fori_loop(0, slot_end, first_pass, (start_top, start_total))
    lse = row_top + jnp.log(row_total)

    def second_pass(slot_at, state_now):
        grad_query, grad_key, grad_value, grad_bias = state_now
        scores, allowed, chosen, matched, key_taken = slot_scores(slot_at)
        value_taken = jnp.take(value_blocks, chosen, axis=0)
        probs = jnp.where(allowed & row_valid[:, :, None], jnp.exp(scores - lse[:, :, None]), 0.0)
        dprobs = jnp.einsum(
            "qid,qjd->qij", grad_blocks, value_taken, preferred_element_type=jnp.float32
        )
        dscores = probs * (dprobs - delta_blocks[:, :, None])
        probs_half = probs.astype(jnp.bfloat16)
        dscores_half = dscores.astype(jnp.bfloat16)
        grad_query = grad_query + jnp.einsum(
            "qij,qjd->qid", dscores_half, key_taken, preferred_element_type=jnp.float32
        )
        key_terms = jnp.einsum(
            "qij,qid->qjd", dscores_half, query_blocks, preferred_element_type=jnp.float32
        )
        value_terms = jnp.einsum(
            "qij,qid->qjd", probs_half, grad_blocks, preferred_element_type=jnp.float32
        )
        grad_key = grad_key.at[chosen].add(key_terms)
        grad_value = grad_value.at[chosen].add(value_terms)
        block_sums = jnp.sum(dscores, axis=(1, 2))
        grad_bias = grad_bias + jnp.sum(jnp.where(matched, block_sums[:, None], 0.0), axis=0)
        return (grad_query, grad_key, grad_value, grad_bias)

    zero_field = jnp.zeros((nblocks, block, head_dim), jnp.float32)
    start_state = (zero_field, zero_field, zero_field, jnp.zeros((nblocks,), jnp.float32))
    grad_query, grad_key, grad_value, grad_bias = lax.fori_loop(
        0, slot_end, second_pass, start_state
    )
    grad_query = (grad_query * scale).reshape(hits, head_dim).astype(jnp.bfloat16)
    grad_key = (grad_key * scale).reshape(hits, head_dim).astype(jnp.bfloat16)
    grad_value = grad_value.reshape(hits, head_dim).astype(jnp.bfloat16)
    return (grad_query, grad_key, grad_value, grad_bias)


def on_device(query, key, value, out_ctx, d_out, score_bias, block_list, block_count, hit_count):
    groups = lax.axis_size("seq")
    tok_rows = query.shape[1]
    width = query.shape[2]
    heads_here = score_bias.shape[0]
    heads_all = heads_here * groups
    head_dim = width // heads_all
    first_row = lax.axis_index("seq") * tok_rows
    hit_limit = hit_count[0]
    row_valid = first_row + jnp.arange(tok_rows, dtype=jnp.int32) < hit_limit
    grad_kept = jnp.where(row_valid[:, None], d_out[0], jnp.zeros((), jnp.bfloat16))

    def split_heads(field):
        return field.reshape(tok_rows, heads_all, head_dim)

    query_heads, key_heads, value_heads, out_heads, grad_heads = (
        lax.all_to_all(split_heads(query[0]), "seq", split_axis=1, concat_axis=0, tiled=True),
        lax.all_to_all(split_heads(key[0]), "seq", split_axis=1, concat_axis=0, tiled=True),
        lax.all_to_all(split_heads(value[0]), "seq", split_axis=1, concat_axis=0, tiled=True),
        lax.all_to_all(split_heads(out_ctx[0]), "seq", split_axis=1, concat_axis=0, tiled=True),
        lax.all_to_all(split_heads(grad_kept), "seq", split_axis=1, concat_axis=0, tiled=True),
    )
    delta_heads = jnp.sum(grad_heads.astype(jnp.float32) * out_heads.astype(jnp.float32), axis=2)
    count_row = block_count[0]
    grad_query, grad_key, grad_value, grad_bias = head_grads(
        query_heads[:, 0],
        key_heads[:, 0],
        value_heads[:, 0],
        grad_heads[:, 0],
        delta_heads[:, 0],
        score_bias[0],
        block_list[0],
        count_row,
        hit_limit,
        block_list.shape[2],
    )
    query_grads = [grad_query]
    key_grads = [grad_key]
    value_grads = [grad_value]
    bias_grads = [grad_bias]
    query_back, key_back, value_back = (
        lax.all_to_all(
            jnp.stack(query_grads, axis=1), "seq", split_axis=0, concat_axis=1, tiled=True
        ),
        lax.all_to_all(
            jnp.stack(key_grads, axis=1), "seq", split_axis=0, concat_axis=1, tiled=True
        ),
        lax.all_to_all(
            jnp.stack(value_grads, axis=1), "seq", split_axis=0, concat_axis=1, tiled=True
        ),
    )
    bias_total = lax.psum(jnp.stack(bias_grads, axis=0), "dp")
    return (
        query_back.reshape(1, tok_rows, width),
        key_back.reshape(1, tok_rows, width),
        value_back.reshape(1, tok_rows, width),
        bias_total,
    )


def solution(mesh):
    placed = (
        P("dp", "seq", None),
        P("dp", "seq", None),
        P("dp", "seq", None),
        P("dp", "seq", None),
        P("dp", "seq", None),
        P("seq", None),
        P("seq", None, None),
        P("seq", None),
        P("dp"),
    )
    return jax.shard_map(
        on_device,
        mesh=mesh,
        in_specs=placed,
        out_specs=(
            P("dp", "seq", None),
            P("dp", "seq", None),
            P("dp", "seq", None),
            P("seq", None),
        ),
        check_vma=False,
    )
```

profile of v0, /device:TPU:0, one launch (start us, length us, event | category | flops | bytes accessed | tf_op | source)
XLA Modules:
  0.0 120.0 jit_solution(9918450063467983925)
XLA Ops:
  0.6 1.7 %copy.95 = bf16[1,128,512]{1,2,0:T(8,128)(2,1)} copy(bf16[1,128,512]{2,1,0:T(8,128)(2,1)} %param.15) | data formatting | bytes 262144 | tf_op args[0]
  2.3 6.5 %all-to-all-start.1 = ((bf16[128,4,128]{0,2,1:T(8,128)(2,1)}), bf16[128,4,128]{0,2,1:T(8,128)(2,1)S(1)}, u32[]{:S(2)}, u32[]{:S(2)}) async-start(bf16[128,4,128]{0,2,1:T(8,128)(2,1)} %bitcast.7), calls=%async_computation.1 | async-start | bytes 262144 | tf_op jit(solution)/shard_map/all_to_all | solution.py:116
  8.8 0.8 copy.94
  9.5 5.3 %all-to-all-done.1 = bf16[128,4,128]{0,2,1:T(8,128)(2,1)S(1)} async-done(((bf16[128,4,128]{0,2,1:T(8,128)(2,1)}), bf16[128,4,128]{0,2,1:T(8,128)(2,1)S(1)}, u32[]{:S(2)}, u32[]{:S(2)}) %all-to-all-start.1) | async-done | bytes 131104 | tf_op jit(solution)/shard_map/all_to_all | solution.py:116
  14.9 3.5 %all-to-all-start = ((bf16[128,4,128]{0,2,1:T(8,128)(2,1)}), bf16[128,4,128]{0,2,1:T(8,128)(2,1)S(1)}, u32[]{:S(2)}, u32[]{:S(2)}) async-start(bf16[128,4,128]{0,2,1:T(8,128)(2,1)} %bitcast.3), calls=%async_computation | async-start | bytes 262144 | tf_op jit(solution)/shard_map/all_to_all | solution.py:117
  19.1 0.8 copy.99
  20.0 0.8 copy.101
  21.1 3.1 %all-to-all-done = bf16[128,4,128]{0,2,1:T(8,128)(2,1)S(1)} async-done(((bf16[128,4,128]{0,2,1:T(8,128)(2,1)}), bf16[128,4,128]{0,2,1:T(8,128)(2,1)S(1)}, u32[]{:S(2)}, u32[]{:S(2)}) %all-to-all-start) | async-done | bytes 131104 | tf_op jit(solution)/shard_map/all_to_all | solution.py:117
  24.2 3.3 %all-to-all-start.2 = ((bf16[128,4,128]{0,2,1:T(8,128)(2,1)}), bf16[128,4,128]{0,2,1:T(8,128)(2,1)S(1)}, u32[]{:S(2)}, u32[]{:S(2)}) async-start(bf16[128,4,128]{0,2,1:T(8,128)(2,1)} %bitcast.15), calls=%async_computation.2 | async-start | bytes 262144 | tf_op jit(solution)/shard_map/all_to_all | solution.py:118
  27.5 0.7 broadcast_select_fusion.4
  28.5 4.9 %all-to-all-done.2 = bf16[128,4,128]{0,2,1:T(8,128)(2,1)S(1)} async-done(((bf16[128,4,128]{0,2,1:T(8,128)(2,1)}), bf16[128,4,128]{0,2,1:T(8,128)(2,1)S(1)}, u32[]{:S(2)}, u32[]{:S(2)}) %all-to-all-start.2) | async-done | bytes 131104 | tf_op jit(solution)/shard_map/all_to_all | solution.py:118
  33.4 3.3 %all-to-all-start.3 = ((bf16[128,4,128]{0,2,1:T(8,128)(2,1)}), bf16[128,4,128]{0,2,1:T(8,128)(2,1)S(1)}, u32[]{:S(2)}, u32[]{:S(2)}) async-start(bf16[128,4,128]{0,2,1:T(8,128)(2,1)} %broadcast_select_fusion.4), calls=%async_computation.3 | async-start | bytes 262144 | tf_op jit(solution)/shard_map/all_to_all | solution.py:120
  37.4 7.7 %while.38 = (s32[]{:T(128)}, f32[4,128]{1,0:T(4,128)S(1)}, f32[4,128]{1,0:T(4,128)S(1)}, s32[4]{0:T(128)S(1)}, s32[4,4]{0,1:T(4,128)S(1)}, /*index=5*/s32[]{:T(1...) while((s32[]{:T(128)}, f32[4,128]{1,0:T(4,128)S(1)}, ...), condition=%wide.region_4.6_spmd.clone, body=%wide.region_0.5_spmd.clone.sunk | while | flops 17241176 | bytes 1081720 | solution.py:60
  37.5 0.7 fusion.83
  39.4 0.7 fusion.83
  41.3 0.7 fusion.83
  43.2 0.7 fusion.83
  45.2 5.1 %all-to-all-start.4 = ((bf16[128,4,128]{0,2,1:T(8,128)(2,1)}), bf16[128,4,128]{0,2,1:T(8,128)(2,1)S(1)}, u32[]{:S(2)}, u32[]{:S(2)}) async-start(bf16[128,4,128]{0,2,1:T(8,128)(2,1)} %bitcast.24), calls=%async_computation.4 | async-start | bytes 262144 | tf_op jit(solution)/shard_map/all_to_all | solution.py:119
  50.5 5.8 %all-to-all-done.4 = bf16[128,4,128]{0,2,1:T(8,128)(2,1)S(1)} async-done(((bf16[128,4,128]{0,2,1:T(8,128)(2,1)}), bf16[128,4,128]{0,2,1:T(8,128)(2,1)S(1)}, u32[]{:S(2)}, u32[]{:S(2)}) %all-to-all-start.4) | async-done | bytes 131104 | tf_op jit(solution)/shard_map/all_to_all | solution.py:119
  56.3 23.8 %while.39 = (s32[]{:T(128)}, f32[4,128,128]{2,1,0:T(8,128)S(1)}, f32[4,128,128]{2,1,0:T(8,128)S(1)}, f32[4,128,128]{2,1,0:T(8,128)S(1)}, f32[4]{0:T(128)S(1)}, /...) while((s32[]{:T(128)}, f32[4,128,128]{2,1,0:T(8,128)S(1)}, ...), condition=%wide.region_12.14_spmd.clone.clone.clone, body=%wide.region_6.0_spmd.clone.clone.clone.sunk | while | flops 85068952 | bytes 5253752 | solution.py:91
  57.3 0.7 fusion.95
  60.3 0.8 scatter_fusion.1
  61.5 0.8 scatter_fusion
  63.2 0.7 fusion.95
  66.3 0.8 scatter_fusion.1
  67.5 0.8 scatter_fusion
  68.3 0.7 fusion.96
  69.2 0.7 fusion.95
  72.2 0.7 scatter_fusion.1
  73.5 0.7 scatter_fusion
  75.1 0.7 fusion.95
  78.2 0.7 scatter_fusion.1
  79.4 0.7 scatter_fusion
  80.7 0.7 reduce.4
  81.4 0.7 reshape.270
  82.1 3.3 %all-to-all-start.7 = ((bf16[4,2,8192]{2,1,0:T(2,128)(2,1)}), bf16[4,2,8192]{2,1,0:T(2,128)(2,1)S(1)}, u32[]{:S(2)}, u32[]{:S(2)}) async-start(bf16[4,2,8192]{2,1,0:T(2,128)(2,1)} %reshape.270), calls=%async_computation.7 | async-start | bytes 262144 | tf_op jit(solution)/shard_map/all_to_all | solution.py:147
  85.5 0.7 reduce.3
  86.2 0.7 reshape.268
  86.9 4.5 %all-to-all-done.7 = bf16[4,2,8192]{2,1,0:T(2,128)(2,1)S(1)} async-done(((bf16[4,2,8192]{2,1,0:T(2,128)(2,1)}), bf16[4,2,8192]{2,1,0:T(2,128)(2,1)S(1)}, u32[]{:S(2)}, u32[]{:S(2)}) %all-to-all-start.7) | async-done | bytes 131104 | tf_op jit(solution)/shard_map/all_to_all | solution.py:147
  91.3 3.3 %all-to-all-start.6 = ((bf16[4,2,8192]{2,1,0:T(2,128)(2,1)}), bf16[4,2,8192]{2,1,0:T(2,128)(2,1)S(1)}, u32[]{:S(2)}, u32[]{:S(2)}) async-start(bf16[4,2,8192]{2,1,0:T(2,128)(2,1)} %reshape.268), calls=%async_computation.6 | async-start | bytes 262144 | tf_op jit(solution)/shard_map/all_to_all | solution.py:144
  94.7 0.7 reduce.2
  95.3 0.7 reshape.266
  96.0 4.6 %all-to-all-done.6 = bf16[4,2,8192]{2,1,0:T(2,128)(2,1)S(1)} async-done(((bf16[4,2,8192]{2,1,0:T(2,128)(2,1)}), bf16[4,2,8192]{2,1,0:T(2,128)(2,1)S(1)}, u32[]{:S(2)}, u32[]{:S(2)}) %all-to-all-start.6) | async-done | bytes 131104 | tf_op jit(solution)/shard_map/all_to_all | solution.py:144
  100.6 3.9 %all-to-all-start.5 = ((bf16[4,2,8192]{2,1,0:T(2,128)(2,1)}), bf16[4,2,8192]{2,1,0:T(2,128)(2,1)S(1)}, u32[]{:S(2)}, u32[]{:S(2)}) async-start(bf16[4,2,8192]{2,1,0:T(2,128)(2,1)} %reshape.266), calls=%async_computation.5 | async-start | bytes 262144 | tf_op jit(solution)/shard_map/all_to_all | solution.py:141
  104.5 12.3 %psum.7 = f32[1,4]{1,0:T(1,128)} all-reduce(f32[1,4]{1,0:T(1,128)S(1)} %bitcast.144), channel_id=1, replica_groups=mesh['dp'=8,'seq'=4] {'dp'}, use_global_device_ids=true, to_apply=%region_13.15 | all-reduce | flops 4 | bytes 32 | tf_op jit(solution)/shard_map/psum | solution.py:151
  117.1 0.8 copy.115
  118.2 0.8 copy.114
  119.2 0.8 copy.113
  (154 shorter events, 21.6 us)
Async XLA Ops:
  2.3 6.5 %copy-start = (bf16[1,128,512]{2,1,0:T(8,128)(2,1)S(1)}, bf16[1,128,512]{2,1,0:T(8,128)(2,1)}, u32[]{:S(2)}) copy-start(bf16[1,128,512]{2,1,0:T(8,128)(2,1)} %param.16) | copy-start | bytes 393220
  2.3 12.6 %all-to-all-start.1 = ((bf16[128,4,128]{0,2,1:T(8,128)(2,1)}), bf16[128,4,128]{0,2,1:T(8,128)(2,1)S(1)}, u32[]{:S(2)}, u32[]{:S(2)}) async-start(bf16[128,4,128]{0,2,1:T(8,128)(2,1)} %bitcast.7), calls=%async_computation.1 | async-start | bytes 262144 | tf_op jit(solution)/shard_map/all_to_all | solution.py:116
  14.8 4.3 %copy-start.1 = (bf16[1,128,512]{2,1,0:T(8,128)(2,1)S(1)}, bf16[1,128,512]{2,1,0:T(8,128)(2,1)}, u32[]{:S(2)}) copy-start(bf16[1,128,512]{2,1,0:T(8,128)(2,1)} %param.17) | copy-start | bytes 393220
  14.9 9.4 %all-to-all-start = ((bf16[128,4,128]{0,2,1:T(8,128)(2,1)}), bf16[128,4,128]{0,2,1:T(8,128)(2,1)S(1)}, u32[]{:S(2)}, u32[]{:S(2)}) async-start(bf16[128,4,128]{0,2,1:T(8,128)(2,1)} %bitcast.3), calls=%async_computation | async-start | bytes 262144 | tf_op jit(solution)/shard_map/all_to_all | solution.py:117
  18.4 0.7 copy-start.5
  19.1 0.9 copy-start.2
  20.0 0.9 copy-start.3
  24.2 9.2 %all-to-all-start.2 = ((bf16[128,4,128]{0,2,1:T(8,128)(2,1)}), bf16[128,4,128]{0,2,1:T(8,128)(2,1)S(1)}, u32[]{:S(2)}, u32[]{:S(2)}) async-start(bf16[128,4,128]{0,2,1:T(8,128)(2,1)} %bitcast.15), calls=%async_computation.2 | async-start | bytes 262144 | tf_op jit(solution)/shard_map/all_to_all | solution.py:118
  33.4 11.8 %all-to-all-start.3 = ((bf16[128,4,128]{0,2,1:T(8,128)(2,1)}), bf16[128,4,128]{0,2,1:T(8,128)(2,1)S(1)}, u32[]{:S(2)}, u32[]{:S(2)}) async-start(bf16[128,4,128]{0,2,1:T(8,128)(2,1)} %broadcast_select_fusion.4), calls=%async_computation.3 | async-start | bytes 262144 | tf_op jit(solution)/shard_map/all_to_all | solution.py:120
  36.8 0.7 copy-start.4
  36.8 0.7 copy-start.6
  45.2 11.0 %all-to-all-start.4 = ((bf16[128,4,128]{0,2,1:T(8,128)(2,1)}), bf16[128,4,128]{0,2,1:T(8,128)(2,1)S(1)}, u32[]{:S(2)}, u32[]{:S(2)}) async-start(bf16[128,4,128]{0,2,1:T(8,128)(2,1)} %bitcast.24), calls=%async_computation.4 | async-start | bytes 262144 | tf_op jit(solution)/shard_map/all_to_all | solution.py:119
  82.1 9.2 %all-to-all-start.7 = ((bf16[4,2,8192]{2,1,0:T(2,128)(2,1)}), bf16[4,2,8192]{2,1,0:T(2,128)(2,1)S(1)}, u32[]{:S(2)}, u32[]{:S(2)}) async-start(bf16[4,2,8192]{2,1,0:T(2,128)(2,1)} %reshape.270), calls=%async_computation.7 | async-start | bytes 262144 | tf_op jit(solution)/shard_map/all_to_all | solution.py:147
  91.3 9.3 %all-to-all-start.6 = ((bf16[4,2,8192]{2,1,0:T(2,128)(2,1)}), bf16[4,2,8192]{2,1,0:T(2,128)(2,1)S(1)}, u32[]{:S(2)}, u32[]{:S(2)}) async-start(bf16[4,2,8192]{2,1,0:T(2,128)(2,1)} %reshape.268), calls=%async_computation.6 | async-start | bytes 262144 | tf_op jit(solution)/shard_map/all_to_all | solution.py:144
  100.6 18.3 %all-to-all-start.5 = ((bf16[4,2,8192]{2,1,0:T(2,128)(2,1)}), bf16[4,2,8192]{2,1,0:T(2,128)(2,1)S(1)}, u32[]{:S(2)}, u32[]{:S(2)}) async-start(bf16[4,2,8192]{2,1,0:T(2,128)(2,1)} %reshape.266), calls=%async_computation.5 | async-start | bytes 262144 | tf_op jit(solution)/shard_map/all_to_all | solution.py:141
where the time goes:
time: 121 us; the launch traced here: 120 us
  starting transfers between devices  32.2 us (27%)
  waiting for transfers between devices  28.2 us (23%)
  other arithmetic  19.7 us (16%)
  local copies, waits for them, and re-layouts  18.3 us (15%)
  blocking collectives  12.3 us (10%)
  matrix products  7.08 us (6%)
  between operations  1.57 us (1%)
    psum x1, blocking collectives, on_device(): bias_total = lax.psum(jnp.stack(bias_grads, axis=0), 'dp')  12.3 us
    unnamed x36, local copies, waits for them, and re-layouts  10.5 us
    all_to_all x1, starting transfers between devices, on_device(): lax.all_to_all(split_heads(query[0]), 'seq', split_axis=1, concat_axis=0,...  6.48 us
    all_to_all x1, waiting for transfers between devices, on_device(): lax.all_to_all(split_heads(out_ctx[0]), 'seq', split_axis=1, concat_axis=...  5.77 us
    and x8, other arithmetic, slot_scores(): allowed = (slot_at < count_row)[:, None, None] & key_real[:, None, :]  5.77 us
    all_to_all x1, waiting for transfers between devices, on_device(): lax.all_to_all(split_heads(query[0]), 'seq', split_axis=1, concat_axis=0,...  5.31 us
    all_to_all x1, starting transfers between devices, on_device(): lax.all_to_all(split_heads(out_ctx[0]), 'seq', split_axis=1, concat_axis=...  5.07 us
    all_to_all x1, waiting for transfers between devices, on_device(): lax.all_to_all(split_heads(value[0]), 'seq', split_axis=1, concat_axis=0,...  4.94 us
  transfers between devices with their start and end apart: 8, of which 6 were waited for; matrix products, arithmetic and copies ran while one was open for 13% of the time, Pallas kernels for 0%

commit v1 on v0

--- a/solution.py
+++ b/solution.py
@@ -5,6 +5,33 @@
 from jax.sharding import PartitionSpec as P
 
 MASKED = -1000000000.0
+
+
+def order_slot(xin, ndim_at, field_in):
+    z_new, r_now = (xin.shape[:ndim_at], xin.shape[ndim_at + 1 :])
+    part_next = jnp.moveaxis(xin.reshape(*z_new, field_in, -1, *r_now), ndim_at, 0)
+    return part_next
+
+
+def push_slot(m, dim_no):
+    high = list(m.shape[1:])
+    high[dim_no] *= m.shape[0]
+    y1 = jnp.moveaxis(m, 0, dim_no).reshape(high)
+    return y1
+
+
+def _cover_digits(base_x, shard_axis, block_here, u):
+    raw_out, z2 = (lax.axis_size(shard_axis), lax.axis_index(shard_axis))
+    out_arr = order_slot(base_x, block_here, raw_out)
+    inbox = [out_arr[z2]]
+    for kk in [*range(1, raw_out)]:
+        e_now = out_arr[z2 ^ kk]
+        n_now = lax.ppermute(e_now, shard_axis, [(b, b ^ kk) for b in range(raw_out)])
+        inbox.append(n_now)
+    latest = jnp.stack(inbox)
+    out_arr = latest[z2 ^ jnp.arange(raw_out)]
+    tmp = push_slot(out_arr, u)
+    return tmp
 
 
 def head_grads(
@@ -144,9 +171,7 @@
         lax.all_to_all(
             jnp.stack(key_grads, axis=1), "seq", split_axis=0, concat_axis=1, tiled=True
         ),
-        lax.all_to_all(
-            jnp.stack(value_grads, axis=1), "seq", split_axis=0, concat_axis=1, tiled=True
-        ),
+        _cover_digits(jnp.stack(value_grads, axis=1), shard_axis="seq", block_here=0, u=1),
     )
     bias_total = lax.psum(jnp.stack(bias_grads, axis=0), "dp")
     return (

time: 121 us -> 114 us (0.942)
  waiting for transfers between devices: 28.2 us -> 18.5 us
  starting transfers between devices: 32.2 us -> 34.5 us
    all_to_all x1, waiting for transfers between devices: 4.62 us -> 0.01 us  [on_device(): lax.all_to_all(jnp.stack(key_grads, axis=1), 'seq', split_axis=0, concat_...]
    ppermute x0 -> x3, starting transfers between devices: none -> 4.49 us  [_cover_digits(): lax.ppermute(e_now, shard_axis, [(b, b ^ kk) for b in range(raw_out)])]
    all_to_all x1 -> x0, waiting for transfers between devices: 4.45 us -> none  [on_device(): lax.all_to_all(jnp.stack(value_grads, axis=1), 'seq', split_axis=0, conca...]
    all_to_all x1 -> x0, starting transfers between devices: 3.33 us -> none  [on_device(): lax.all_to_all(jnp.stack(value_grads, axis=1), 'seq', split_axis=0, conca...]
    all_to_all x1, starting transfers between devices: 3.46 us -> 6.48 us  [on_device(): lax.all_to_all(split_heads(key[0]), 'seq', split_axis=1, concat_axis=0, t...]
    all_to_all x1, starting transfers between devices: 6.48 us -> 3.46 us  [on_device(): lax.all_to_all(split_heads(query[0]), 'seq', split_axis=1, concat_axis=0,...]
    all_to_all x1, waiting for transfers between devices: 5.31 us -> 2.48 us  [on_device(): lax.all_to_all(split_heads(query[0]), 'seq', split_axis=1, concat_axis=0,...]
    all_to_all x1, waiting for transfers between devices: 3.11 us -> 5.31 us  [on_device(): lax.all_to_all(split_heads(key[0]), 'seq', split_axis=1, concat_axis=0, t...]
  transfers between devices with their start and end apart: 8 -> 10, of which waited for: 6 -> 4; matrix products, arithmetic and copies ran while one was open for 13% -> 13% of each run, Pallas kernels for 0% -> 0%
where the time goes in v1:
time: 114 us; the launch traced here: 112 us
  starting transfers between devices  34.5 us (30%)
  other arithmetic  19.1 us (17%)
  local copies, waits for them, and re-layouts  18.7 us (16%)
  waiting for transfers between devices  18.5 us (16%)
  blocking collectives  12.3 us (11%)
  matrix products  7.06 us (6%)
  between operations  1.57 us (1%)
    psum x1, blocking collectives, on_device(): bias_total = lax.psum(jnp.stack(bias_grads, axis=0), 'dp')  12.3 us
    unnamed x33, local copies, waits for them, and re-layouts  10.3 us
    all_to_all x1, starting transfers between devices, on_device(): lax.all_to_all(split_heads(key[0]), 'seq', split_axis=1, concat_axis=0, t...  6.48 us
    all_to_all x1, waiting for transfers between devices, on_device(): lax.all_to_all(split_heads(out_ctx[0]), 'seq', split_axis=1, concat_axis=...  5.77 us
    and x8, other arithmetic, slot_scores(): allowed = (slot_at < count_row)[:, None, None] & key_real[:, None, :]  5.77 us
    all_to_all x1, waiting for transfers between devices, on_device(): lax.all_to_all(split_heads(key[0]), 'seq', split_axis=1, concat_axis=0, t...  5.31 us
    all_to_all x1, starting transfers between devices, on_device(): lax.all_to_all(split_heads(out_ctx[0]), 'seq', split_axis=1, concat_axis=...  5.07 us
    all_to_all x1, starting transfers between devices, on_device(): lax.all_to_all(jnp.stack(key_grads, axis=1), 'seq', split_axis=0, concat_...  5.01 us
  transfers between devices with their start and end apart: 10, of which 4 were waited for; matrix products, arithmetic and copies ran while one was open for 13% of the time, Pallas kernels for 0%

profile of v1, /device:TPU:0, one launch (start us, length us, event | category | flops | bytes accessed | tf_op | source)
XLA Modules:
  0.0 112.4 jit_solution(13548269285631254748)
XLA Ops:
  0.6 1.7 %copy.93 = bf16[1,128,512]{1,2,0:T(8,128)(2,1)} copy(bf16[1,128,512]{2,1,0:T(8,128)(2,1)} %param.16) | data formatting | bytes 262144 | tf_op args[1]
  2.3 6.5 %all-to-all-start = ((bf16[128,4,128]{0,2,1:T(8,128)(2,1)}), bf16[128,4,128]{0,2,1:T(8,128)(2,1)S(1)}, u32[]{:S(2)}, u32[]{:S(2)}) async-start(bf16[128,4,128]{0,2,1:T(8,128)(2,1)} %bitcast.3), calls=%async_computation | async-start | bytes 262144 | tf_op jit(solution)/shard_map/all_to_all | solution.py:144
  8.8 0.8 copy.94
  9.5 5.3 %all-to-all-done = bf16[128,4,128]{0,2,1:T(8,128)(2,1)S(1)} async-done(((bf16[128,4,128]{0,2,1:T(8,128)(2,1)}), bf16[128,4,128]{0,2,1:T(8,128)(2,1)S(1)}, u32[]{:S(2)}, u32[]{:S(2)}) %all-to-all-start) | async-done | bytes 131104 | tf_op jit(solution)/shard_map/all_to_all | solution.py:144
  14.9 3.5 %all-to-all-start.1 = ((bf16[128,4,128]{0,2,1:T(8,128)(2,1)}), bf16[128,4,128]{0,2,1:T(8,128)(2,1)S(1)}, u32[]{:S(2)}, u32[]{:S(2)}) async-start(bf16[128,4,128]{0,2,1:T(8,128)(2,1)} %bitcast.7), calls=%async_computation.1 | async-start | bytes 262144 | tf_op jit(solution)/shard_map/all_to_all | solution.py:143
  18.4 0.7 copy-done.5
  19.2 0.8 copy.98
  21.0 0.8 copy.100
  21.7 2.5 %all-to-all-done.1 = bf16[128,4,128]{0,2,1:T(8,128)(2,1)S(1)} async-done(((bf16[128,4,128]{0,2,1:T(8,128)(2,1)}), bf16[128,4,128]{0,2,1:T(8,128)(2,1)S(1)}, u32[]{:S(2)}, u32[]{:S(2)}) %all-to-all-start.1) | async-done | bytes 131104 | tf_op jit(solution)/shard_map/all_to_all | solution.py:143
  24.2 3.3 %all-to-all-start.2 = ((bf16[128,4,128]{0,2,1:T(8,128)(2,1)}), bf16[128,4,128]{0,2,1:T(8,128)(2,1)S(1)}, u32[]{:S(2)}, u32[]{:S(2)}) async-start(bf16[128,4,128]{0,2,1:T(8,128)(2,1)} %bitcast.15), calls=%async_computation.2 | async-start | bytes 262144 | tf_op jit(solution)/shard_map/all_to_all | solution.py:145
  27.5 0.7 broadcast_select_fusion.4
  28.5 4.9 %all-to-all-done.2 = bf16[128,4,128]{0,2,1:T(8,128)(2,1)S(1)} async-done(((bf16[128,4,128]{0,2,1:T(8,128)(2,1)}), bf16[128,4,128]{0,2,1:T(8,128)(2,1)S(1)}, u32[]{:S(2)}, u32[]{:S(2)}) %all-to-all-start.2) | async-done | bytes 131104 | tf_op jit(solution)/shard_map/all_to_all | solution.py:145
  33.4 3.3 %all-to-all-start.3 = ((bf16[128,4,128]{0,2,1:T(8,128)(2,1)}), bf16[128,4,128]{0,2,1:T(8,128)(2,1)S(1)}, u32[]{:S(2)}, u32[]{:S(2)}) async-start(bf16[128,4,128]{0,2,1:T(8,128)(2,1)} %broadcast_select_fusion.4), calls=%async_computation.3 | async-start | bytes 262144 | tf_op jit(solution)/shard_map/all_to_all | solution.py:147
  37.4 7.7 %while.38 = (s32[]{:T(128)}, f32[4,128]{1,0:T(4,128)S(1)}, f32[4,128]{1,0:T(4,128)S(1)}, s32[4]{0:T(128)S(1)}, s32[4,4]{0,1:T(4,128)S(1)}, /*index=5*/s32[]{:T(1...) while((s32[]{:T(128)}, f32[4,128]{1,0:T(4,128)S(1)}, ...), condition=%wide.region_4.6_spmd.clone, body=%wide.region_0.5_spmd.clone.sunk | while | flops 17241176 | bytes 1081720 | solution.py:87
  38.2 0.7 fusion.84
  40.2 0.7 fusion.84
  42.1 0.7 fusion.84
  44.0 0.7 fusion.84
  45.3 5.1 %all-to-all-start.4 = ((bf16[128,4,128]{0,2,1:T(8,128)(2,1)}), bf16[128,4,128]{0,2,1:T(8,128)(2,1)S(1)}, u32[]{:S(2)}, u32[]{:S(2)}) async-start(bf16[128,4,128]{0,2,1:T(8,128)(2,1)} %bitcast.24), calls=%async_computation.4 | async-start | bytes 262144 | tf_op jit(solution)/shard_map/all_to_all | solution.py:146
  50.5 5.8 %all-to-all-done.4 = bf16[128,4,128]{0,2,1:T(8,128)(2,1)S(1)} async-done(((bf16[128,4,128]{0,2,1:T(8,128)(2,1)}), bf16[128,4,128]{0,2,1:T(8,128)(2,1)S(1)}, u32[]{:S(2)}, u32[]{:S(2)}) %all-to-all-start.4) | async-done | bytes 131104 | tf_op jit(solution)/shard_map/all_to_all | solution.py:146
  56.4 23.8 %while.39 = (s32[]{:T(128)}, f32[4,128,128]{2,1,0:T(8,128)S(1)}, f32[4,128,128]{2,1,0:T(8,128)S(1)}, f32[4,128,128]{2,1,0:T(8,128)S(1)}, f32[4]{0:T(128)S(1)}, /...) while((s32[]{:T(128)}, f32[4,128,128]{2,1,0:T(8,128)S(1)}, ...), condition=%wide.region_12.14_spmd.clone.clone.clone, body=%wide.region_6.0_spmd.clone.clone.clone.sunk | while | flops 85068952 | bytes 5253752 | solution.py:118
  56.6 0.7 fusion.96
  57.3 0.7 fusion.97
  60.6 0.8 scatter_fusion
  61.5 0.8 scatter_fusion.1
  62.6 0.7 fusion.96
  63.3 0.7 fusion.97
  66.5 0.8 scatter_fusion
  67.4 0.8 scatter_fusion.1
  68.5 0.7 fusion.96
  69.3 0.7 fusion.97
  72.5 0.7 scatter_fusion
  73.4 0.7 scatter_fusion.1
  74.5 0.7 fusion.96
  75.2 0.7 fusion.97
  78.4 0.7 scatter_fusion
  79.3 0.7 scatter_fusion.1
  80.8 0.7 reduce.2
  81.5 0.7 reshape.285
  82.1 3.3 %all-to-all-start.5 = ((bf16[4,2,8192]{2,1,0:T(2,128)(2,1)}), bf16[4,2,8192]{2,1,0:T(2,128)(2,1)S(1)}, u32[]{:S(2)}, u32[]{:S(2)}) async-start(bf16[4,2,8192]{2,1,0:T(2,128)(2,1)} %reshape.285), calls=%async_computation.5 | async-start | bytes 262144 | tf_op jit(solution)/shard_map/all_to_all | solution.py:168
  85.5 0.7 reduce.3
  86.2 0.7 reshape.287
  86.9 3.8 %collective-permute-start.2 = (bf16[128,1,128]{2,0,1:T(8,128)(2,1)S(1)}, bf16[128,1,128]{2,0,1:T(8,128)(2,1)S(1)}, u32[]{:S(2)}, u32[]{:S(2)}) collective-permute-start(bf16[128,1,128]{2,0,1:T(8,128)(2,1)S(1)} %get-tuple-element.870), channel_id=1, source_target_pairs={{0,3},{1,2},{2,1},{3,0},{4,7},{5,6},{6,5},{7,4},{8,11},{9,10},{10,... | collective-permute-start | bytes 98312 | tf_op jit(solution)/shard_map/ppermute | solution.py:29
  91.4 5.0 %all-to-all-start.6 = ((bf16[4,2,8192]{2,1,0:T(2,128)(2,1)}), bf16[4,2,8192]{2,1,0:T(2,128)(2,1)S(1)}, u32[]{:S(2)}, u32[]{:S(2)}) async-start(bf16[4,2,8192]{2,1,0:T(2,128)(2,1)} %reshape.287), calls=%async_computation.6 | async-start | bytes 262144 | tf_op jit(solution)/shard_map/all_to_all | solution.py:171
  96.4 12.3 %psum.7 = f32[1,4]{1,0:T(1,128)} all-reduce(f32[1,4]{1,0:T(1,128)S(1)} %bitcast.160), channel_id=1, replica_groups=mesh['dp'=8,'seq'=4] {'dp'}, use_global_device_ids=true, to_apply=%region_13.15 | all-reduce | flops 4 | bytes 32 | tf_op jit(solution)/shard_map/psum | solution.py:176
  109.5 0.8 copy.113
  110.6 0.8 copy.111
  111.7 0.8 copy.112
  (159 shorter events, 20.8 us)
Async XLA Ops:
  2.3 6.5 %copy-start = (bf16[1,128,512]{2,1,0:T(8,128)(2,1)S(1)}, bf16[1,128,512]{2,1,0:T(8,128)(2,1)}, u32[]{:S(2)}) copy-start(bf16[1,128,512]{2,1,0:T(8,128)(2,1)} %param.15) | copy-start | bytes 393220
  2.3 12.6 %all-to-all-start = ((bf16[128,4,128]{0,2,1:T(8,128)(2,1)}), bf16[128,4,128]{0,2,1:T(8,128)(2,1)S(1)}, u32[]{:S(2)}, u32[]{:S(2)}) async-start(bf16[128,4,128]{0,2,1:T(8,128)(2,1)} %bitcast.3), calls=%async_computation | async-start | bytes 262144 | tf_op jit(solution)/shard_map/all_to_all | solution.py:144
  14.8 4.3 %copy-start.1 = (bf16[1,128,512]{2,1,0:T(8,128)(2,1)S(1)}, bf16[1,128,512]{2,1,0:T(8,128)(2,1)}, u32[]{:S(2)}) copy-start(bf16[1,128,512]{2,1,0:T(8,128)(2,1)} %param.17) | copy-start | bytes 393220
  14.9 9.4 %all-to-all-start.1 = ((bf16[128,4,128]{0,2,1:T(8,128)(2,1)}), bf16[128,4,128]{0,2,1:T(8,128)(2,1)S(1)}, u32[]{:S(2)}, u32[]{:S(2)}) async-start(bf16[128,4,128]{0,2,1:T(8,128)(2,1)} %bitcast.7), calls=%async_computation.1 | async-start | bytes 262144 | tf_op jit(solution)/shard_map/all_to_all | solution.py:143
  18.4 0.7 copy-start.5
  19.2 0.9 copy-start.2
  20.1 0.9 copy-start.3
  24.2 9.2 %all-to-all-start.2 = ((bf16[128,4,128]{0,2,1:T(8,128)(2,1)}), bf16[128,4,128]{0,2,1:T(8,128)(2,1)S(1)}, u32[]{:S(2)}, u32[]{:S(2)}) async-start(bf16[128,4,128]{0,2,1:T(8,128)(2,1)} %bitcast.15), calls=%async_computation.2 | async-start | bytes 262144 | tf_op jit(solution)/shard_map/all_to_all | solution.py:145
  33.4 11.9 %all-to-all-start.3 = ((bf16[128,4,128]{0,2,1:T(8,128)(2,1)}), bf16[128,4,128]{0,2,1:T(8,128)(2,1)S(1)}, u32[]{:S(2)}, u32[]{:S(2)}) async-start(bf16[128,4,128]{0,2,1:T(8,128)(2,1)} %broadcast_select_fusion.4), calls=%async_computation.3 | async-start | bytes 262144 | tf_op jit(solution)/shard_map/all_to_all | solution.py:147
  36.8 0.7 copy-start.4
  36.8 0.7 copy-start.6
  45.3 11.0 %all-to-all-start.4 = ((bf16[128,4,128]{0,2,1:T(8,128)(2,1)}), bf16[128,4,128]{0,2,1:T(8,128)(2,1)S(1)}, u32[]{:S(2)}, u32[]{:S(2)}) async-start(bf16[128,4,128]{0,2,1:T(8,128)(2,1)} %bitcast.24), calls=%async_computation.4 | async-start | bytes 262144 | tf_op jit(solution)/shard_map/all_to_all | solution.py:146
  82.1 9.3 %all-to-all-start.5 = ((bf16[4,2,8192]{2,1,0:T(2,128)(2,1)}), bf16[4,2,8192]{2,1,0:T(2,128)(2,1)S(1)}, u32[]{:S(2)}, u32[]{:S(2)}) async-start(bf16[4,2,8192]{2,1,0:T(2,128)(2,1)} %reshape.285), calls=%async_computation.5 | async-start | bytes 262144 | tf_op jit(solution)/shard_map/all_to_all | solution.py:168
  86.9 21.9 %collective-permute-start.2 = (bf16[128,1,128]{2,0,1:T(8,128)(2,1)S(1)}, bf16[128,1,128]{2,0,1:T(8,128)(2,1)S(1)}, u32[]{:S(2)}, u32[]{:S(2)}) collective-permute-start(bf16[128,1,128]{2,0,1:T(8,128)(2,1)S(1)} %get-tuple-element.870), channel_id=1, source_target_pairs={{0,3},{1,2},{2,1},{3,0},{4,7},{5,6},{6,5},{7,4},{8,11},{9,10},{10,... | collective-permute-start | bytes 98312 | tf_op jit(solution)/shard_map/ppermute | solution.py:29
  90.8 18.0 %collective-permute-start.1 = (bf16[128,1,128]{2,0,1:T(8,128)(2,1)S(1)}, bf16[128,1,128]{2,0,1:T(8,128)(2,1)S(1)}, u32[]{:S(2)}, u32[]{:S(2)}) collective-permute-start(bf16[128,1,128]{2,0,1:T(8,128)(2,1)S(1)} %get-tuple-element.871), channel_id=1, source_target_pairs={{0,2},{1,3},{2,0},{3,1},{4,6},{5,7},{6,4},{7,5},{8,10},{9,11},{10,... | collective-permute-start | bytes 98312 | tf_op jit(solution)/shard_map/ppermute | solution.py:29
  90.8 18.0 %collective-permute-start = (bf16[128,1,128]{2,0,1:T(8,128)(2,1)S(1)}, bf16[128,1,128]{2,0,1:T(8,128)(2,1)S(1)}, u32[]{:S(2)}, u32[]{:S(2)}) collective-permute-start(bf16[128,1,128]{2,0,1:T(8,128)(2,1)S(1)} %get-tuple-element.872), channel_id=1, source_target_pairs={{0,1},{1,0},{2,3},{3,2},{4,5},{5,4},{6,7},{7,6},{8,9},{9,8},{10,11... | collective-permute-start | bytes 98312 | tf_op jit(solution)/shard_map/ppermute | solution.py:29
  91.4 20.0 %all-to-all-start.6 = ((bf16[4,2,8192]{2,1,0:T(2,128)(2,1)}), bf16[4,2,8192]{2,1,0:T(2,128)(2,1)S(1)}, u32[]{:S(2)}, u32[]{:S(2)}) async-start(bf16[4,2,8192]{2,1,0:T(2,128)(2,1)} %reshape.287), calls=%async_computation.6 | async-start | bytes 262144 | tf_op jit(solution)/shard_map/all_to_all | solution.py:171
